TPU v7x, 512 devices: a whole 4x8x8 slice. The times are simulated.
512 devices in a mesh: dp: 16 (over y, core), expert: 32 (over z, x).
Axes of the slice: x: 4, y: 8, z: 8, core: 2. Of those that a mesh axis runs over, the one named last changes fastest.
Arguments:
- queries: bfloat16 [16, 4096, 2048], P('dp', 'expert'), may hold values from -5.5 to 5.5
- keys: bfloat16 [16, 4096, 2048], P('dp', 'expert'), may hold values from -5.5 to 5.5
- values: bfloat16 [16, 4096, 2048], P('dp', 'expert'), may hold values from -6 to 6
- doc_ids: int32 [16, 4096], P('dp', 'expert'), may hold values from 0 to 7, never falling along the last dimension, each value on 1 to 1024 neighbouring positions
- expert_index: int32 [16, 4096, 2], P('dp', 'expert'), may hold values from 0 to 31, all different within a row; in each aligned block of 128 rows (0 to 127, 128 to 255, ..., all dimensions but the last counted through in order) at most 12 rows name the same one
- gates: float32 [16, 4096, 2], P('dp', 'expert'), may hold values from 0.1 to 1
- capacity: int32 [32], replicated, may hold values from 6 to 12, as said below
- norm_gain: float32 [2048], replicated, may hold values from 0.1 to 1.9
- gate_weight: bfloat16 [32, 2048, 1024], P('expert', 'dp'), may hold values from -0.125 to 0.125
- up_weight: bfloat16 [32, 2048, 1024], P('expert', 'dp'), may hold values from -0.125 to 0.125
- down_weight: bfloat16 [32, 1024, 2048], P('expert', 'dp'), may hold values from -0.1875 to 0.1875
Outputs:
- mixed: bfloat16 [16, 4096, 2048], P('dp', 'expert')
Inputs may be any that keep to these rules, and one draw needn't show every extreme that they name: `doc_ids`: never falls along a window; each protein has 1 to 1024 residues, one exactly 1024; every number of proteins below 8 appears. `expert_index`: the two experts of a residue differ; within the 128 residues of one device (aligned blocks of a window) no expert is named by more than 12 residues, a bound that some block reaches. Some expert has capacity exactly 12.
All inputs are finite; a program needn't handle non-finite values.
Results may differ from a plain program's by a relative error of at most 0.017.
Values may be sent and summed in bfloat16 or wider, within the bound.
A program may use at most 64 MiB of HBM per device.

v0:
```python
import math

import jax
import jax.numpy as jnp
from jax import lax
from jax.sharding import PartitionSpec as P

HEAD_DIM = 128
TOP = 2
WINDOW = 512


def shifted_2(block, axis, distance):
    devices = range(lax.axis_size(axis))
    route = [(i - distance, i) for i in devices if i - distance in devices]
    return lax.ppermute(block, axis, route)


def attend_local(queries, key_rows, value_rows, query_docs, key_docs, query_start, key_start):
    rows_dev, width = queries.shape
    heads = width // HEAD_DIM
    q_block = min(512, rows_dev)
    before = key_rows.shape[0] - rows_dev

    def one_block(number):
        begin = number * q_block
        query_part = queries.reshape(q_block, heads, HEAD_DIM)
        key_part = key_rows.reshape(before + q_block, heads, HEAD_DIM)
        value_part = value_rows.reshape(before + q_block, heads, HEAD_DIM)
        query_pos = query_start + begin + jnp.arange(q_block, dtype=jnp.int32)
        key_pos = key_start + begin + jnp.arange(before + q_block, dtype=jnp.int32)
        allowed = (key_pos[None, :] <= query_pos[:, None]) & (
            key_pos[None, :] > query_pos[:, None] - WINDOW
        )
        allowed = allowed & (key_pos[None, :] >= 0) & (key_docs[None, :] == query_docs[:, None])
        scores = jnp.einsum(
            "qhd,khd->hqk", query_part, key_part, preferred_element_type=jnp.float32
        ) * (1.0 / math.sqrt(HEAD_DIM))
        scores = jnp.where(allowed[None], scores, -1e30)
        highest = jnp.max(scores, axis=-1, keepdims=True)
        expo = jnp.exp(scores - highest)
        probs = (expo / jnp.sum(expo, axis=-1, keepdims=True)).astype(jnp.bfloat16)
        result = jnp.einsum("hqk,khd->qhd", probs, value_part, preferred_element_type=jnp.float32)
        return result.reshape(q_block, width).astype(jnp.bfloat16)

    blocks = lax.map(one_block, jnp.arange(rows_dev // q_block, dtype=jnp.int32))
    return blocks.reshape(rows_dev, width)


def per_device(
    queries,
    keys,
    values,
    doc_ids,
    expert_index,
    gates,
    capacity,
    norm_gain,
    gate_weight,
    up_weight,
    down_weight,
):
    rows_dev = queries.shape[1]
    width = queries.shape[2]
    reach_back = (WINDOW - 1) // rows_dev + 1
    own_pair = jnp.stack([keys[0], values[0]], axis=0)
    own_docs = doc_ids[0].astype(jnp.bfloat16)
    earlier = []
    for number in range(reach_back):
        earlier.insert(0, shifted_2((own_pair, own_docs), "expert", number + 1))
    pair_all = jnp.concatenate([shifted[0] for shifted in earlier] + [own_pair], axis=1)
    docs_all = jnp.concatenate([shifted[1] for shifted in earlier] + [own_docs], axis=0)
    position = lax.axis_index("expert")
    attended = attend_local(
        queries[0],
        pair_all[0],
        pair_all[1],
        own_docs,
        docs_all,
        position * rows_dev,
        (position - reach_back) * rows_dev,
    )
    flat_att = attended.astype(jnp.float32)
    normed = (
        flat_att
        * lax.rsqrt(jnp.mean(flat_att * flat_att, axis=-1, keepdims=True) + 1e-05)
        * norm_gain
    ).astype(jnp.bfloat16)
    experts = lax.axis_size("expert")
    most = max(2, 3 * rows_dev * TOP // (2 * experts))
    chosen_flat = expert_index[0].reshape(-1)
    onehot = (chosen_flat[:, None] == jnp.arange(experts, dtype=jnp.int32)[None, :]).astype(
        jnp.int32
    )
    ranks = jnp.sum(onehot * (jnp.cumsum(onehot, axis=0) - 1), axis=1)
    limits = jnp.sum(onehot * capacity[None, :], axis=1)
    kept = ranks < limits
    slot = jnp.where(kept, chosen_flat * most + ranks, experts * most)
    token_of = jnp.arange(rows_dev * TOP, dtype=jnp.int32) // TOP
    slot_token = jnp.full((experts * most,), -1, jnp.int32).at[slot].set(token_of, mode="drop")
    filled = slot_token >= 0
    outgoing = jnp.where(
        filled[:, None], normed[jnp.maximum(slot_token, 0)], jnp.zeros((), jnp.bfloat16)
    )
    outgoing = outgoing.reshape(experts, most, width)
    received = lax.all_to_all(outgoing, "expert", split_axis=0, concat_axis=0, tiled=True)
    sources = received.shape[0]
    flat_rows = received.reshape(sources * most, width)
    columns = flat_rows
    gate_sum = jnp.dot(
        columns,
        lax.all_gather(gate_weight, "dp", axis=1, tiled=True)[0],
        preferred_element_type=jnp.float32,
    )
    up_sum = jnp.dot(
        columns,
        lax.all_gather(up_weight, "dp", axis=1, tiled=True)[0],
        preferred_element_type=jnp.float32,
    )
    hidden = (jax.nn.silu(gate_sum) * up_sum).astype(jnp.bfloat16)
    columns = hidden
    result = jnp.dot(
        columns,
        lax.all_gather(down_weight, "dp", axis=1, tiled=True)[0],
        preferred_element_type=jnp.float32,
    )
    answered = result.astype(jnp.bfloat16).reshape(sources, most, width)
    returned = lax.all_to_all(answered, "expert", split_axis=0, concat_axis=0, tiled=True)
    back_flat = returned.reshape(experts * most, width)
    picked = back_flat[jnp.minimum(slot, experts * most - 1)].reshape(rows_dev, TOP, width)
    weight = jnp.where(kept, gates[0].reshape(-1), 0.0).reshape(rows_dev, TOP)
    combined = flat_att
    for which in range(TOP):
        combined = combined + picked[:, which].astype(jnp.float32) * weight[:, which : which + 1]
    return combined.astype(jnp.bfloat16)[None]


def solution(mesh):
    placed = (
        P("dp", "expert", None),
        P("dp", "expert", None),
        P("dp", "expert", None),
        P("dp", "expert"),
        P("dp", "expert", None),
        P("dp", "expert", None),
        P(),
        P(),
        P("expert", "dp", None),
        P("expert", "dp", None),
        P("expert", "dp", None),
    )
    return jax.shard_map(
        per_device, mesh=mesh, in_specs=placed, out_specs=P("dp", "expert", None), check_vma=False
    )
```

profile of v0, /device:TPU:1, one launch (start us, length us, event | category | flops | bytes accessed | tf_op | source)
XLA Modules:
  0.0 280.7 jit_solution(13630439240030400420)
XLA Ops:
  6.5 0.7 all-gather.4.cloned.1.call-update
  7.3 0.0 all-gather.6.cloned.1.call-start
  7.3 0.7 all-gather.6.cloned.1.call-update
  8.0 0.0 all-gather.8.cloned.1.call-start
  8.1 0.7 convert_bitcast_fusion
  8.7 4.8 %collective-permute-start.4 = (bf16[128]{0:T(256)(128)(2,1)S(1)}, bf16[128]{0:T(256)(128)(2,1)S(1)}, u32[]{:S(2)}, u32[]{:S(2)}) collective-permute-start(bf16[128]{0:T(256)(128)(2,1)S(1)} %convert_bitcast_fusion), channel_id=1, source_target_pairs={{0,4},{1,5},{2,6},{3,7},{4,8},{5,9},{6,10},{7,11},{8,12},{9,13},{1... | collective-permute-start | bytes 776 | tf_op jit(solution)/shard_map/ppermute | solution.py:16
  13.5 4.4 %collective-permute-start.5 = (bf16[128]{0:T(256)(128)(2,1)S(1)}, bf16[128]{0:T(256)(128)(2,1)S(1)}, u32[]{:S(2)}, u32[]{:S(2)}) collective-permute-start(bf16[128]{0:T(256)(128)(2,1)S(1)} %convert_bitcast_fusion), channel_id=1, source_target_pairs={{0,3},{1,4},{2,5},{3,6},{4,7},{5,8},{6,9},{7,10},{8,11},{9,12},{10... | collective-permute-start | bytes 776 | tf_op jit(solution)/shard_map/ppermute | solution.py:16
  17.9 1.3 copy.33
  19.3 1.3 copy.34
  20.6 0.1 pad_maximum_fusion
  20.7 5.1 %collective-permute-start = (bf16[2,128,2048]{1,2,0:T(8,128)(2,1)S(1)}, bf16[2,128,2048]{1,2,0:T(8,128)(2,1)}, u32[]{:S(2)}, u32[]{:S(2)}) collective-permute-start(bf16[2,128,2048]{1,2,0:T(8,128)(2,1)S(1)} %pad_maximum_fusion), channel_id=1, source_target_pairs={{0,4},{1,5},{2,6},{3,7},{4,8},{5,9},{6,10},{7,11},{8,12},{9,13},{1... | collective-permute-start | bytes 3145736 | tf_op jit(solution)/shard_map/ppermute | solution.py:16
  25.7 5.2 %collective-permute-start.1 = (bf16[2,128,2048]{1,2,0:T(8,128)(2,1)S(1)}, bf16[2,128,2048]{1,2,0:T(8,128)(2,1)}, u32[]{:S(2)}, u32[]{:S(2)}) collective-permute-start(bf16[2,128,2048]{1,2,0:T(8,128)(2,1)S(1)} %pad_maximum_fusion), channel_id=1, source_target_pairs={{0,3},{1,4},{2,5},{3,6},{4,7},{5,8},{6,9},{7,10},{8,11},{9,12},{10... | collective-permute-start | bytes 3145736 | tf_op jit(solution)/shard_map/ppermute | solution.py:16
  31.0 5.1 %collective-permute-start.2 = (bf16[2,128,2048]{1,2,0:T(8,128)(2,1)S(1)}, bf16[2,128,2048]{1,2,0:T(8,128)(2,1)}, u32[]{:S(2)}, u32[]{:S(2)}) collective-permute-start(bf16[2,128,2048]{1,2,0:T(8,128)(2,1)S(1)} %pad_maximum_fusion), channel_id=1, source_target_pairs={{0,2},{1,3},{2,4},{3,5},{4,6},{5,7},{6,8},{7,9},{8,10},{9,11},{10,... | collective-permute-start | bytes 3145736 | tf_op jit(solution)/shard_map/ppermute | solution.py:16
  36.1 0.1 copy.38
  36.2 0.1 eq.56
  36.4 0.1 eq.52
  36.6 0.6 reduce-window.6
  37.2 0.2 slice_reduce_fusion.2
  37.4 0.1 copy.41
  37.5 0.1 mul.117
  37.7 0.1 select_reduce_fusion
  37.8 1.4 scatter_custom_fusion
  39.3 2.5 collective-permute-start.3
  41.8 3.6 %collective-permute-start.6 = (bf16[128]{0:T(256)(128)(2,1)S(1)}, bf16[128]{0:T(256)(128)(2,1)S(1)}, u32[]{:S(2)}, u32[]{:S(2)}) collective-permute-start(bf16[128]{0:T(256)(128)(2,1)S(1)} %convert_bitcast_fusion), channel_id=1, source_target_pairs={{0,2},{1,3},{2,4},{3,5},{4,6},{5,7},{6,8},{7,9},{8,10},{9,11},{10,... | collective-permute-start | bytes 776 | tf_op jit(solution)/shard_map/ppermute | solution.py:16
  45.5 0.1 copy.52
  45.6 0.1 broadcast_in_dim.77
  45.7 32.7 %collective-permute-done.6 = bf16[128]{0:T(256)(128)(2,1)S(1)} collective-permute-done((bf16[128]{0:T(256)(128)(2,1)S(1)}, bf16[128]{0:T(256)(128)(2,1)S(1)}, u32[]{:S(2)}, u32[]{:S(2)}) %collective-permute-start.6) | collective-permute-done | bytes 288 | tf_op jit(solution)/shard_map/ppermute | solution.py:16
  78.4 1.5 collective-permute-start.7
  79.8 0.2 dynamic-update-slice
  80.1 0.2 dynamic-update-slice.1
  80.2 0.2 dynamic-update-slice.2
  80.4 0.2 dynamic-update-slice.3
  80.6 0.2 dynamic-update-slice.4
  80.8 0.3 compare_and_fusion
  81.2 1.4 constant_dynamic-update-slice_fusion.4
  82.6 1.5 constant_dynamic-update-slice_fusion.3
  84.1 1.5 constant_dynamic-update-slice_fusion.2
  85.6 1.5 constant_dynamic-update-slice_fusion.1
  87.1 0.2 constant_dynamic-update-slice_fusion
  87.4 0.5 fusion.35
  87.8 0.9 fusion.25
  88.7 2.4 fusion.37
  91.1 0.9 multiply_reduce_fusion
  92.0 0.3 copy.42
  92.4 0.2 multiply_convert_fusion.1
  92.5 3.1 %gather_fusion = bf16[384,2048]{1,0:T(8,128)(2,1)} fusion(bf16[128,2048]{1,0:T(8,128)(2,1)S(1)} %multiply_convert_fusion.1, s32[1024]{0:T(1024)S(1)} %pad_clamp_fusion.1), kind=kCustom, calls=%fused_computation | custom fusion | bytes 3147264 | tf_op jit(solution)/shard_map/gather | solution.py:103
  95.6 2.4 gather.9
  98.0 0.2 broadcast_select_fusion
  98.2 95.8 %all_to_all.10 = bf16[32,12,2048]{2,1,0:T(8,128)(2,1)S(1)} all-to-all(bf16[32,12,2048]{2,1,0:T(8,128)(2,1)S(1)} %broadcast_select_fusion), channel_id=1, replica_groups=mesh['dp'=16,'expert'=32] {'expert'}, dimensions={0} | all-to-all | bytes 3145728 | tf_op jit(solution)/shard_map/all_to_all | solution.py:106
  194.0 1.3 reshape.359
  195.4 5.8 %fusion.5 = f32[384,1024]{1,0:T(8,128)} fusion(bf16[384,2048]{1,0:T(8,128)(2,1)} %reshape.359, bf16[1,2048,1024]{2,1,0:T(8,128)(2,1)} %all-gather.4.cloned.1.call-done), kind=kOutput, calls=%fused_computation.11 | convolution fusion | flops 1610612736 | bytes 7340032 | tf_op jit(solution)/shard_map/dot_general | solution.py:110
  201.1 8.6 %fusion.8 = bf16[384,2048]{1,0:T(8,128)(2,1)} fusion(bf16[1,1024,2048]{2,1,0:T(8,128)(2,1)} %all-gather.8.cloned.1.call-done, f32[384,1024]{1,0:T(8,128)} %fusion.5, bf16[384,2048]{1,0:T(8,128)(2,1)S(1)} %copy-done.1, bf16[1,2048,1024]{2,1,0:T(8,128)(2,1)} %all-gather.6.cloned.1.call-done), kind=kOutput, calls=%fused_computation.14 | convolution fusion | flops 3224371200 | bytes 13107200 | tf_op jit(solution)/shard_map/dot_general | solution.py:122
  209.8 3.6 %reshape.360 = bf16[32,12,2048]{2,1,0:T(8,128)(2,1)} reshape(bf16[384,2048]{1,0:T(8,128)(2,1)} %fusion.8) | data formatting | bytes 3145728 | tf_op jit(solution)/shard_map/reshape | solution.py:127
  213.3 7.1 %all-to-all-start.1 = ((bf16[32,12,2048]{2,1,0:T(8,128)(2,1)}), bf16[32,12,2048]{2,1,0:T(8,128)(2,1)}, u32[]{:S(2)}, u32[]{:S(2)}) async-start(bf16[32,12,2048]{2,1,0:T(8,128)(2,1)} %reshape.360), calls=%async_computation.1 | async-start | bytes 4194304 | tf_op jit(solution)/shard_map/all_to_all | solution.py:128
  220.4 0.2 lt.46
  220.6 0.1 copy.44
  220.7 0.2 slice_reduce_fusion.1
  220.9 1.3 copy.45
  222.2 43.9 %all-to-all-done.1 = bf16[32,12,2048]{2,1,0:T(8,128)(2,1)} async-done(((bf16[32,12,2048]{2,1,0:T(8,128)(2,1)}), bf16[32,12,2048]{2,1,0:T(8,128)(2,1)}, u32[]{:S(2)}, u32[]{:S(2)}) %all-to-all-start.1) | async-done | bytes 1572896 | tf_op jit(solution)/shard_map/all_to_all | solution.py:128
  266.2 2.5 reshape.361
  268.7 1.4 gather_fusion.1
  270.1 0.7 reshape.362
  270.8 1.5 fusion.36
  272.3 1.9 fusion.20
  (44 shorter events, 0.2 us)
Async XLA Ops:
  6.5 29.6 %copy-start.4 = (s32[1,128,2]{1,2,0:T(2,128)S(1)}, s32[1,128,2]{1,2,0:T(2,128)}, u32[]{:S(2)}) copy-start(s32[1,128,2]{1,2,0:T(2,128)} %param.15) | copy-start | bytes 3076
  6.5 188.8 %all-gather.4.cloned.1.call-start = ((), (), s32[]{:S(2)}) async-start(), calls=%async_computation.2 | async-start | bytes 4456448 | tf_op jit(solution)/shard_map/all_gather | solution.py:112
  7.3 30.4 %copy-start.6 = (s32[32]{0:T(128)S(1)}, s32[32]{0:T(128)}, u32[]{:S(2)}) copy-start(s32[32]{0:T(128)} %param.17) | copy-start | bytes 388
  7.3 38.2 %copy-start.2 = (bf16[1,128,2048]{2,1,0:T(8,128)(2,1)S(1)}, bf16[1,128,2048]{2,1,0:T(8,128)(2,1)}, u32[]{:S(2)}) copy-start(bf16[1,128,2048]{2,1,0:T(8,128)(2,1)} %param.11) | copy-start | bytes 1572868
  7.3 193.9 %all-gather.6.cloned.1.call-start = ((), (), s32[]{:S(2)}) async-start(), calls=%async_computation.3 | async-start | bytes 4456448 | tf_op jit(solution)/shard_map/all_gather | solution.py:117
  8.0 193.1 %all-gather.8.cloned.1.call-start = ((), (), s32[]{:S(2)}) async-start(), calls=%async_computation.4 | async-start | bytes 4456448 | tf_op jit(solution)/shard_map/all_gather | solution.py:124
  8.7 30.5 %collective-permute-start.4 = (bf16[128]{0:T(256)(128)(2,1)S(1)}, bf16[128]{0:T(256)(128)(2,1)S(1)}, u32[]{:S(2)}, u32[]{:S(2)}) collective-permute-start(bf16[128]{0:T(256)(128)(2,1)S(1)} %convert_bitcast_fusion), channel_id=1, source_target_pairs={{0,4},{1,5},{2,6},{3,7},{4,8},{5,9},{6,10},{7,11},{8,12},{9,13},{1... | collective-permute-start | bytes 776 | tf_op jit(solution)/shard_map/ppermute | solution.py:16
  13.5 28.3 %collective-permute-start.5 = (bf16[128]{0:T(256)(128)(2,1)S(1)}, bf16[128]{0:T(256)(128)(2,1)S(1)}, u32[]{:S(2)}, u32[]{:S(2)}) collective-permute-start(bf16[128]{0:T(256)(128)(2,1)S(1)} %convert_bitcast_fusion), channel_id=1, source_target_pairs={{0,3},{1,4},{2,5},{3,6},{4,7},{5,8},{6,9},{7,10},{8,11},{9,12},{10... | collective-permute-start | bytes 776 | tf_op jit(solution)/shard_map/ppermute | solution.py:16
  20.7 60.5 %collective-permute-start = (bf16[2,128,2048]{1,2,0:T(8,128)(2,1)S(1)}, bf16[2,128,2048]{1,2,0:T(8,128)(2,1)}, u32[]{:S(2)}, u32[]{:S(2)}) collective-permute-start(bf16[2,128,2048]{1,2,0:T(8,128)(2,1)S(1)} %pad_maximum_fusion), channel_id=1, source_target_pairs={{0,4},{1,5},{2,6},{3,7},{4,8},{5,9},{6,10},{7,11},{8,12},{9,13},{1... | collective-permute-start | bytes 3145736 | tf_op jit(solution)/shard_map/ppermute | solution.py:16
  25.7 56.9 %collective-permute-start.1 = (bf16[2,128,2048]{1,2,0:T(8,128)(2,1)S(1)}, bf16[2,128,2048]{1,2,0:T(8,128)(2,1)}, u32[]{:S(2)}, u32[]{:S(2)}) collective-permute-start(bf16[2,128,2048]{1,2,0:T(8,128)(2,1)S(1)} %pad_maximum_fusion), channel_id=1, source_target_pairs={{0,3},{1,4},{2,5},{3,6},{4,7},{5,8},{6,9},{7,10},{8,11},{9,12},{10... | collective-permute-start | bytes 3145736 | tf_op jit(solution)/shard_map/ppermute | solution.py:16
  31.0 53.1 %collective-permute-start.2 = (bf16[2,128,2048]{1,2,0:T(8,128)(2,1)S(1)}, bf16[2,128,2048]{1,2,0:T(8,128)(2,1)}, u32[]{:S(2)}, u32[]{:S(2)}) collective-permute-start(bf16[2,128,2048]{1,2,0:T(8,128)(2,1)S(1)} %pad_maximum_fusion), channel_id=1, source_target_pairs={{0,2},{1,3},{2,4},{3,5},{4,6},{5,7},{6,8},{7,9},{8,10},{9,11},{10,... | collective-permute-start | bytes 3145736 | tf_op jit(solution)/shard_map/ppermute | solution.py:16
  39.3 46.3 %collective-permute-start.3 = (bf16[2,128,2048]{1,2,0:T(8,128)(2,1)S(1)}, bf16[2,128,2048]{1,2,0:T(8,128)(2,1)}, u32[]{:S(2)}, u32[]{:S(2)}) collective-permute-start(bf16[2,128,2048]{1,2,0:T(8,128)(2,1)S(1)} %pad_maximum_fusion), channel_id=1, source_target_pairs={{0,1},{1,2},{2,3},{3,4},{4,5},{5,6},{6,7},{7,8},{8,9},{9,10},{10,1... | collective-permute-start | bytes 3145736 | tf_op jit(solution)/shard_map/ppermute | solution.py:16
  41.8 36.5 %collective-permute-start.6 = (bf16[128]{0:T(256)(128)(2,1)S(1)}, bf16[128]{0:T(256)(128)(2,1)S(1)}, u32[]{:S(2)}, u32[]{:S(2)}) collective-permute-start(bf16[128]{0:T(256)(128)(2,1)S(1)} %convert_bitcast_fusion), channel_id=1, source_target_pairs={{0,2},{1,3},{2,4},{3,5},{4,6},{5,7},{6,8},{7,9},{8,10},{9,11},{10,... | collective-permute-start | bytes 776 | tf_op jit(solution)/shard_map/ppermute | solution.py:16
  78.4 2.1 collective-permute-start.7
  91.1 1.2 copy-start.3
  195.4 5.8 %copy-start.1 = (bf16[384,2048]{1,0:T(8,128)(2,1)S(1)}, bf16[384,2048]{1,0:T(8,128)(2,1)}, u32[]{:S(2)}) copy-start(bf16[384,2048]{1,0:T(8,128)(2,1)} %reshape.359) | copy-start | bytes 4718596
  213.3 7.3 %copy-start.5 = (f32[1,128,2]{1,2,0:T(2,128)S(1)}, f32[1,128,2]{1,2,0:T(2,128)}, u32[]{:S(2)}) copy-start(f32[1,128,2]{1,2,0:T(2,128)} %param.16) | copy-start | bytes 3076
  213.3 52.8 %all-to-all-start.1 = ((bf16[32,12,2048]{2,1,0:T(8,128)(2,1)}), bf16[32,12,2048]{2,1,0:T(8,128)(2,1)}, u32[]{:S(2)}, u32[]{:S(2)}) async-start(bf16[32,12,2048]{2,1,0:T(8,128)(2,1)} %reshape.360), calls=%async_computation.1 | async-start | bytes 4194304 | tf_op jit(solution)/shard_map/all_to_all | solution.py:128
  270.8 1.5 copy-start
Sparse Core Ops, SparseCore 0:
  9.5 50.2 all-gather.3
  61.8 43.1 all-gather.5
  107.2 43.1 all-gather.7
where the time goes:
time: 286 us; the launch traced here: 281 us
  blocking collectives  95.8 us (33%)
  waiting for transfers between devices  78 us (27%)
  starting transfers between devices  39.3 us (14%)
  local copies, waits for them, and re-layouts  31 us (11%)
  matrix products  16.2 us (6%)
  between operations  13.6 us (5%)
  other arithmetic  6.77 us (2%)
    all_to_all x1, blocking collectives, per_device(): lax.all_to_all(outgoing, 'expert', split_axis=0, concat_axis=0, tiled=True)  95.8 us
    all_to_all x1, waiting for transfers between devices, per_device(): lax.all_to_all(answered, 'expert', split_axis=0, concat_axis=0, tiled=True)  43.9 us
    ppermute x8, waiting for transfers between devices, shifted_2(): return lax.ppermute(block, axis, route)  32.7 us
    ppermute x8, starting transfers between devices, shifted_2(): return lax.ppermute(block, axis, route)  32.2 us
    unnamed x27, local copies, waits for them, and re-layouts  9.69 us
    dot_general x1, matrix products, per_device(): jnp.dot(columns, lax.all_gather(down_weight, 'dp', axis=1, tiled=True)[0]...  8.61 us
    all_to_all x1, starting transfers between devices, per_device(): lax.all_to_all(answered, 'expert', split_axis=0, concat_axis=0, tiled=True)  7.07 us
    dot_general x1, matrix products, per_device(): jnp.dot(columns, lax.all_gather(gate_weight, 'dp', axis=1, tiled=True)[0]...  5.77 us
  transfers between devices with their start and end apart: 12, of which 2 were waited for; matrix products, arithmetic and copies ran while one was open for 12% of the time, Pallas kernels for 0%

commit v1 on v0

v1 whole, which is shorter than its diff:
```python
import functools
import math

import jax
import jax.numpy as jnp
from jax import lax
from jax.experimental import pallas as pl
from jax.experimental.pallas import tpu as pltpu
from jax.sharding import PartitionSpec as P

HEAD_DIM = 128
TOP = 2
GROUP = 4
MOST = 12
CHUNKS = 2
MESH = pl.DeviceIdType.MESH
BF = jnp.bfloat16
F32 = jnp.float32


def layer_kernel(
    experts,
    dp,
    q_in,
    k_in,
    v_in,
    meta_in,
    cap_in,
    gain_in,
    wg_in,
    wu_in,
    wd_in,
    out,
    qbuf,
    kbuf,
    vbuf,
    metabuf,
    keyrow,
    keycol,
    docrow,
    pick,
    mix,
    att,
    sbuf,
    xbuf,
    hbuf,
    ybuf,
    rbuf,
    fbuf,
    wgf,
    wuf,
    wdf,
    q_sem,
    kv_sem,
    halo_sem,
    meta_sem,
    disp_sem,
    ret_sem,
    fin_sem,
    ring_sem,
    part_sem,
    own_sem,
    qkv_send,
    halo_send,
    meta_send,
    disp_send,
    ret_send,
    fin_send,
    w_send,
):
    rows, width = q_in.shape
    cols = width // GROUP
    chunk = cols // CHUNKS
    heads = chunk // HEAD_DIM
    span = GROUP * rows
    slots = GROUP * MOST
    planes = experts // GROUP
    ring = dp // 2
    hops = ring // 2

    me = lax.axis_index("expert")
    z, x = lax.div(me, GROUP), lax.rem(me, GROUP)
    d = lax.axis_index("dp")
    y, core = lax.div(d, 2), lax.rem(d, 2)
    z_next = lax.rem(z + 1, planes)

    def at(start, size, unit):
        return pl.ds(pl.multiple_of(start, unit), size)

    def send(src, dst, send_sem, recv_sem, where):
        pltpu.make_async_remote_copy(
            src_ref=src, dst_ref=dst, send_sem=send_sem, recv_sem=recv_sem, device_id=where, device_id_type=MESH
        ).start()

    def local(src, dst, sem):
        pltpu.make_async_copy(src, dst, sem).start()

    def wait(ref, sem):
        pltpu.make_async_copy(ref, ref, sem).wait()

    barrier = pltpu.get_barrier_semaphore()

    def greet(i, carry):
        pl.semaphore_signal(barrier, inc=1, device_id={"expert": lax.rem(me + i, experts)}, device_id_type=MESH)
        return carry

    lax.fori_loop(1, experts, greet, 0)
    up, down, partner = lax.rem(y + 1, ring) * 2 + core, lax.rem(y + ring - 1, ring) * 2 + core, y * 2 + 1 - core
    for other in (up, down, partner):
        pl.semaphore_signal(barrier, inc=1, device_id={"dp": other}, device_id_type=MESH)
    pl.semaphore_wait(barrier, experts + 2)

    for i in range(1, GROUP):
        there = z * GROUP + lax.rem(x + i, GROUP)
        send(meta_in, metabuf.at[GROUP + x], meta_send, meta_sem, {"expert": there})
    for i in range(GROUP):
        send(meta_in, metabuf.at[x], meta_send, meta_sem, {"expert": z_next * GROUP + i})

    for c in range(CHUNKS):
        here = pl.ds(c * chunk, chunk)
        for i in range(1, GROUP):
            peer = lax.rem(x + i, GROUP)
            theirs = at(peer * cols + c * chunk, chunk, HEAD_DIM)
            there = {"expert": z * GROUP + peer}
            send(k_in.at[:, theirs], kbuf.at[at(span + x * rows, rows, rows), here], qkv_send.at[1], kv_sem.at[c], there)
            send(v_in.at[:, theirs], vbuf.at[at(span + x * rows, rows, rows), here], qkv_send.at[2], kv_sem.at[c], there)
            send(q_in.at[:, theirs], qbuf.at[at(x * rows, rows, rows), here], qkv_send.at[0], q_sem.at[c], there)
        mine = at(x * cols + c * chunk, chunk, HEAD_DIM)
        local(k_in.at[:, mine], kbuf.at[at(span + x * rows, rows, rows), here], kv_sem.at[c])
        local(v_in.at[:, mine], vbuf.at[at(span + x * rows, rows, rows), here], kv_sem.at[c])
        local(q_in.at[:, mine], qbuf.at[at(x * rows, rows, rows), here], q_sem.at[c])

    weights = ((wg_in, wgf), (wu_in, wuf), (wd_in, wdf))

    def block_of(piece, number, half):
        size = weights[piece][0].shape[0]
        base = (number * 2 + core) * size
        if half is None:
            return at(base, size, size)
        return at(base + half * (size // 2), size // 2, size // 2)

    def half_at(step, way):
        return way if step == hops - 1 else None

    for piece, (w_in, w_full) in enumerate(weights):
        size = w_in.shape[0]
        for way, to in ((0, up), (1, down)):
            half = half_at(0, way)
            source = w_in if half is None else w_in.at[pl.ds(half * (size // 2), size // 2)]
            send(source, w_full.at[block_of(piece, y, half)], w_send.at[piece], ring_sem.at[way, 0, piece], {"dp": to})
        send(w_in, w_full.at[block_of(piece, y, None)], w_send.at[piece], part_sem.at[piece], {"dp": partner})
        local(w_in, w_full.at[block_of(piece, y, None)], own_sem.at[piece])

    def relay(step, piece):
        w_full = weights[piece][1]
        for way, to in ((0, up), (1, down)):
            number = lax.rem(y + ring - step - 1, ring) if way == 0 else lax.rem(y + step + 1, ring)
            came = w_full.at[block_of(piece, number, half_at(step, way))]
            wait(came, ring_sem.at[way, step, piece])
            if step + 1 < hops:
                onward = w_full.at[block_of(piece, number, half_at(step + 1, way))]
                send(onward, onward, w_send.at[piece], ring_sem.at[way, step + 1, piece], {"dp": to})
            send(came, came, w_send.at[piece], part_sem.at[piece], {"dp": partner})

    pending = [(step, piece) for step in range(hops) for piece in range(3)]

    def pump(count):
        for _ in range(count):
            if pending:
                relay(*pending.pop(0))

    metabuf[GROUP + x] = meta_in[...]
    wait(metabuf.at[pl.ds(0, 2 * GROUP - 1)], meta_sem)
    number = lax.broadcasted_iota(jnp.int32, (experts, rows), 0).astype(F32)
    earlier = (
        lax.broadcasted_iota(jnp.int32, (rows, rows), 0) < lax.broadcasted_iota(jnp.int32, (rows, rows), 1)
    ).astype(BF)
    capacity = cap_in[...]
    first = jnp.where(z > 0, 1.0, 0.0)
    for b in range(GROUP):
        block = metabuf[GROUP + b]
        lanes = pl.ds(b * rows, rows)
        chosen = [(block[k : k + 1, :] == number).astype(F32) for k in range(TOP)]
        before = jnp.dot((chosen[0] + chosen[1]).astype(BF), earlier, preferred_element_type=F32)
        for k in range(TOP):
            rank = jnp.sum(chosen[k] * before, axis=0, keepdims=True)
            limit = jnp.sum(chosen[k] * capacity, axis=0, keepdims=True)
            key = jnp.where(rank < limit, block[k : k + 1, :] * slots + b * MOST + rank, -1.0)
            keyrow[pl.ds(k, 1), lanes] = key
        keyrow[pl.ds(2, 3), lanes] = block[2:5, :]
        docrow[pl.ds(0, 1), pl.ds(span + b * rows, rows)] = block[4:5, :]
        docrow[pl.ds(0, 1), lanes] = (metabuf[b, pl.ds(4, 1), :] + 1.0) * first - 1.0
        keycol[pl.ds(b * rows, rows), :] = jnp.transpose(keyrow[:, lanes])

    batch = min(8, experts)
    part = batch * slots

    def build_pick(g, carry):
        there = at(g * part, part, slots)
        row = (lax.broadcasted_iota(jnp.int32, (part, span), 0) + g * part).astype(F32)
        hit = (row == keyrow[0:1, :]) | (row == keyrow[1:2, :])
        pick[there, :] = hit.astype(F32).astype(BF)
        return carry

    lax.fori_loop(0, experts // batch, build_pick, 0)

    def build_mix(b, carry):
        there = at(b * rows, rows, rows)
        slot = lax.broadcasted_iota(jnp.int32, (rows, experts * slots), 1).astype(F32)
        info = keycol[there, :]
        weight = jnp.where(slot == info[:, 0:1], info[:, 2:3], 0.0) + jnp.where(slot == info[:, 1:2], info[:, 3:4], 0.0)
        mix[there, :] = weight.astype(BF)
        return carry

    lax.fori_loop(0, GROUP, build_mix, 0)

    for c in range(CHUNKS):
        here = pl.ds(c * chunk, chunk)
        wait(kbuf.at[:, here], kv_sem.at[c])
        for buf in (kbuf, vbuf):
            send(
                buf.at[pl.ds(span, span), here],
                buf.at[pl.ds(0, span), here],
                halo_send,
                halo_sem.at[c],
                {"expert": z_next * GROUP + x},
            )
        pump(1)

    near = lax.broadcasted_iota(jnp.int32, (rows, span + rows), 0)
    far = lax.broadcasted_iota(jnp.int32, (rows, span + rows), 1)
    band = (far > near) & (far <= near + span)
    scale = 1.0 / math.sqrt(HEAD_DIM)
    for c in range(CHUNKS):
        here = pl.ds(c * chunk, chunk)
        wait(qbuf.at[:, here], q_sem.at[c])
        wait(kbuf.at[:, here], halo_sem.at[c])

        def attend(b, carry):
            there = at(b * rows, rows, rows)
            reach = at(b * rows, span + rows, rows)
            same = docrow[0:1, reach] == keycol[there, :][:, 4:5]
            bias = jnp.where(band & same, 0.0, -1e30)
            for h in range(heads):
                lanes = pl.ds(c * chunk + h * HEAD_DIM, HEAD_DIM)
                scores = lax.dot_general(
                    qbuf[there, lanes], kbuf[reach, lanes], (((1,), (1,)), ((), ())), preferred_element_type=F32
                )
                scores = scores * scale + bias
                expo = jnp.exp(scores - jnp.max(scores, axis=-1, keepdims=True))
                probs = (expo * (1.0 / jnp.sum(expo, axis=-1, keepdims=True))).astype(BF)
                att[there, lanes] = jnp.dot(probs, vbuf[reach, lanes], preferred_element_type=F32).astype(BF)
            return carry

        lax.fori_loop(0, GROUP, attend, 0)

        def select(g, carry):
            there = at(g * part, part, slots)
            sbuf[there, here] = jnp.dot(pick[there, :], att[:, here], preferred_element_type=F32).astype(BF)
            return carry

        lax.fori_loop(0, experts // batch, select, 0)
        pump(1)
        landing = xbuf.at[at(z * slots, slots, slots), at(x * cols + c * chunk, chunk, HEAD_DIM)]

        def dispatch(i, carry):
            e = lax.rem(me + i, experts)
            send(sbuf.at[at(e * slots, slots, slots), here], landing, disp_send, disp_sem.at[c], {"expert": e})
            return carry

        lax.fori_loop(1, experts, dispatch, 0)
        local(sbuf.at[at(me * slots, slots, slots), here], landing, disp_sem.at[c])

    pump(len(pending))
    for c in range(CHUNKS):
        wait(rbuf.at[:, pl.ds(c * chunk, chunk)], disp_sem.at[c])

    gain = gain_in[...]

    def normalise(g, carry):
        there = at(g * slots, slots, slots)
        row = xbuf[there, :].astype(F32)
        inverse = lax.rsqrt(jnp.sum(row * row, axis=-1, keepdims=True) * (1.0 / width) + 1e-05)
        xbuf[there, :] = (row * inverse * gain).astype(BF)
        return carry

    lax.fori_loop(0, planes, normalise, 0)
    for piece in range(2):
        wait(weights[piece][0], own_sem.at[piece])
        wait(weights[piece][1].at[pl.ds(0, width // 2)], part_sem.at[piece])
    hidden = wgf.shape[1]
    strip = min(256, hidden)

    def inner(n, carry):
        there = at(n * strip, strip, strip)
        gate = jnp.dot(xbuf[...], wgf[:, there], preferred_element_type=F32)
        upward = jnp.dot(xbuf[...], wuf[:, there], preferred_element_type=F32)
        hbuf[:, there] = (gate / (1.0 + jnp.exp(-gate)) * upward).astype(BF)
        return carry

    lax.fori_loop(0, hidden // strip, inner, 0)
    wait(wd_in, own_sem.at[2])
    wait(wdf.at[pl.ds(0, hidden // 2)], part_sem.at[2])

    for c in range(CHUNKS):
        here = pl.ds(c * chunk, chunk)
        landing = rbuf.at[at(me * slots, slots, slots), here]

        def outer(j, carry):
            peer = lax.rem(x + 1 + j, GROUP)
            theirs = at(peer * cols + c * chunk, chunk, HEAD_DIM)
            ybuf[:, theirs] = jnp.dot(hbuf[...], wdf[:, theirs], preferred_element_type=F32).astype(BF)

            def give(i, inner_carry):
                plane = lax.rem(z + i, planes)
                e = plane * GROUP + peer
                source = ybuf.at[at(plane * slots, slots, slots), theirs]

                @pl.when(e != me)
                def _():
                    send(source, landing, ret_send, ret_sem.at[c], {"expert": e})

                @pl.when(e == me)
                def _():
                    local(source, landing, ret_sem.at[c])

                return inner_carry

            lax.fori_loop(0, planes, give, 0)
            return carry

        lax.fori_loop(0, GROUP, outer, 0)

    for c in range(CHUNKS):
        here = pl.ds(c * chunk, chunk)
        wait(rbuf.at[:, here], ret_sem.at[c])

        def combine(b, carry):
            there = at(b * rows, rows, rows)
            total = att[there, here].astype(F32) + jnp.dot(mix[there, :], rbuf[:, here], preferred_element_type=F32)
            fbuf[there, here] = total.astype(BF)
            return carry

        lax.fori_loop(0, GROUP, combine, 0)
        landing = out.at[:, at(x * cols + c * chunk, chunk, HEAD_DIM)]
        for i in range(1, GROUP):
            peer = lax.rem(x + i, GROUP)
            send(
                fbuf.at[at(peer * rows, rows, rows), here], landing, fin_send, fin_sem, {"expert": z * GROUP + peer}
            )
        local(fbuf.at[at(x * rows, rows, rows), here], landing, fin_sem)

    for i in range(3):
        wait(qbuf.at[pl.ds(0, span - rows), :], qkv_send.at[i])
        size = weights[i][0].shape[0]
        wait(weights[i][1].at[pl.ds(0, (dp - 1) * size)], w_send.at[i])
    wait(kbuf, halo_send)
    wait(metabuf.at[pl.ds(0, 2 * GROUP - 1)], meta_send)
    wait(rbuf.at[pl.ds(0, (experts - 1) * slots), :], disp_send)
    wait(rbuf.at[pl.ds(0, (experts - 1) * slots), :], ret_send)
    wait(qbuf.at[pl.ds(0, span - rows), :], fin_send)
    wait(out, fin_sem)


def per_device(
    experts,
    dp,
    queries,
    keys,
    values,
    doc_ids,
    expert_index,
    gates,
    capacity,
    norm_gain,
    gate_weight,
    up_weight,
    down_weight,
):
    rows, width = queries.shape[1:]
    hidden = gate_weight.shape[2]
    cols = width // GROUP
    span = GROUP * rows
    slots = GROUP * MOST
    meta = jnp.concatenate(
        [
            expert_index[0].T.astype(F32),
            gates[0].T,
            doc_ids.astype(F32),
            jnp.zeros((8 - 2 * TOP - 1, rows), F32),
        ],
        axis=0,
    )
    limits = jnp.broadcast_to(capacity.astype(F32)[:, None], (experts, rows))
    hbm = pl.BlockSpec(memory_space=pl.ANY)
    vmem = pl.BlockSpec(memory_space=pltpu.VMEM)
    dma = pltpu.SemaphoreType.DMA
    out = pl.pallas_call(
        functools.partial(layer_kernel, experts, dp),
        out_shape=jax.ShapeDtypeStruct((rows, width), BF),
        in_specs=[hbm, hbm, hbm, vmem, vmem, vmem, hbm, hbm, hbm],
        out_specs=hbm,
        scratch_shapes=[
            pltpu.VMEM((span, cols), BF),
            pltpu.VMEM((2 * span, cols), BF),
            pltpu.VMEM((2 * span, cols), BF),
            pltpu.VMEM((2 * GROUP, 8, rows), F32),
            pltpu.VMEM((8, span), F32),
            pltpu.VMEM((span, 8), F32),
            pltpu.VMEM((8, 2 * span), F32),
            pltpu.VMEM((experts * slots, span), BF),
            pltpu.VMEM((span, experts * slots), BF),
            pltpu.VMEM((span, cols), BF),
            pltpu.VMEM((experts * slots, cols), BF),
            pltpu.VMEM((experts // GROUP * slots, width), BF),
            pltpu.VMEM((experts // GROUP * slots, hidden), BF),
            pltpu.VMEM((experts // GROUP * slots, width), BF),
            pltpu.VMEM((experts * slots, cols), BF),
            pltpu.VMEM((span, cols), BF),
            pltpu.VMEM((width, hidden), BF),
            pltpu.VMEM((width, hidden), BF),
            pltpu.VMEM((hidden, width), BF),
            dma((CHUNKS,)),
            dma((CHUNKS,)),
            dma((CHUNKS,)),
            dma,
            dma((CHUNKS,)),
            dma((CHUNKS,)),
            dma,
            dma((2, dp // 4, 3)),
            dma((3,)),
            dma((3,)),
            dma((3,)),
            dma,
            dma,
            dma,
            dma,
            dma,
            dma((3,)),
        ],
        compiler_params=pltpu.CompilerParams(
            collective_id=0, has_side_effects=True, vmem_limit_bytes=56 * 1024 * 1024
        ),
        name="layer",
    )(
        queries[0],
        keys[0],
        values[0],
        meta,
        limits,
        norm_gain[None, :],
        gate_weight[0],
        up_weight[0],
        down_weight[0],
    )
    return out[None]


def solution(mesh):
    placed = (
        P("dp", "expert", None),
        P("dp", "expert", None),
        P("dp", "expert", None),
        P("dp", "expert"),
        P("dp", "expert", None),
        P("dp", "expert", None),
        P(),
        P(),
        P("expert", "dp", None),
        P("expert", "dp", None),
        P("expert", "dp", None),
    )
    body = functools.partial(per_device, mesh.shape["expert"], mesh.shape["dp"])
    return jax.shard_map(body, mesh=mesh, in_specs=placed, out_specs=P("dp", "expert", None), check_vma=False)
```

time: 286 us -> 135 us (0.47); the launches traced: 281 us -> 134 us
  Pallas kernels: 0 us -> 128 us
  blocking collectives: 95.8 us -> 0 us
  waiting for transfers between devices: 78 us -> 0 us
  starting transfers between devices: 39.3 us -> 0 us
  local copies, waits for them, and re-layouts: 31 us -> 5.22 us
  matrix products: 16.2 us -> 0 us
  between operations: 13.6 us -> 0.02 us
  other arithmetic: 6.77 us -> 0.67 us
    pallas_call x0 -> x1, Pallas kernels: none -> 128 us  [per_device(): pl.pallas_call(functools.partial(layer_kernel, experts, dp), out_shape=ja...]
    all_to_all x1 -> x0, blocking collectives: 95.8 us -> none  [per_device(): lax.all_to_all(outgoing, 'expert', split_axis=0, concat_axis=0, tiled=True)]
    all_to_all x1 -> x0, waiting for transfers between devices: 43.9 us -> none  [per_device(): lax.all_to_all(answered, 'expert', split_axis=0, concat_axis=0, tiled=True)]
    ppermute x8 -> x0, waiting for transfers between devices: 32.7 us -> none  [shifted_2(): return lax.ppermute(block, axis, route)]
    ppermute x8 -> x0, starting transfers between devices: 32.2 us -> none  [shifted_2(): return lax.ppermute(block, axis, route)]
    dot_general x4 -> x0, matrix products: 16.2 us -> none  [the longest x1 8.61 us: per_device(): jnp.dot(columns, lax.all_gather(down_weight, 'dp', axis=1, tiled=True)[0]...]
    reshape x4 -> x0, local copies, waits for them, and re-layouts: 8.14 us -> none  [the longest x1 3.59 us: per_device(): answered = result.astype(jnp.bfloat16).reshape(sources, most, width)]
    all_to_all x1 -> x0, starting transfers between devices: 7.07 us -> none  [per_device(): lax.all_to_all(answered, 'expert', split_axis=0, concat_axis=0, tiled=True)]
  transfers between devices with their start and end apart: 12 -> 0, of which waited for: 2 -> 0; matrix products, arithmetic and copies ran while one was open for 12% -> 0% of each run, Pallas kernels for 0% -> 0%
where the time goes in v1:
time: 135 us; the launch traced here: 134 us
  Pallas kernels  128 us (95%)
  local copies, waits for them, and re-layouts  5.22 us (4%)
    pallas_call x1, Pallas kernels, per_device(): pl.pallas_call(functools.partial(layer_kernel, experts, dp), out_shape=ja...  128 us
    unnamed x9, local copies, waits for them, and re-layouts  4.47 us

profile of v1, /device:TPU:1, one launch (start us, length us, event | category | flops | bytes accessed | tf_op | source)
XLA Modules:
  0.0 133.5 jit_solution(17624605921491860844)
XLA Ops:
  0.0 0.0 copy-start.2
  0.0 0.7 copy-done.2
  0.7 0.0 copy-start.3
  0.7 0.7 copy-done.3
  1.3 0.0 copy-start.1
  1.3 0.1 pad.3.clone
  1.4 0.6 copy-done.1
  2.0 0.0 copy-start
  2.0 0.7 copy-done
  2.7 0.7 maximum_maximum_fusion.meta_in
  3.3 0.7 broadcast_in_dim.16.cap_in
  4.0 127.6 %layer.1 = bf16[128,2048]{1,0:T(8,128)(2,1)} custom-call(bf16[128,2048]{1,0:T(8,128)(2,1)} %bitcast.16, bf16[128,2048]{1,0:T(8,128)(2,1)} %bitcast.17, bf16[128,2048]{1,0:T(8,128)(2,1)} %bitcast.18, f32[8,128]{1,0:T(8,128)} %maximum_maximum_fusion.meta_in, f32[32,128]{1,0:T(8,128)} %broadcast_in_dim.16.cap_in, f32[1,2048]{1,0:T(1,128)} %bitcast.22, ...), custom_call_target="tpu_custom_call" | custom-call | tf_op jit(solution)/shard_map/layer/pallas_call | solution.py:398
  131.6 1.9 %copy.13 = bf16[1,128,2048]{2,1,0:T(8,128)(2,1)} copy(bf16[1,128,2048]{2,1,0:T(8,128)(2,1)} %bitcast.15) | data formatting | bytes 1048576
  (4 shorter events, 0.0 us)
Async XLA Ops:
  0.0 0.7 copy-start.2
  0.7 0.7 copy-start.3
  1.3 0.7 copy-start.1
  2.0 0.7 copy-start

commit v2 on v1

v2 whole, which is shorter than its diff:
```python
import functools
import math

import jax
import jax.numpy as jnp
from jax import lax
from jax.experimental import pallas as pl
from jax.experimental.pallas import tpu as pltpu
from jax.sharding import PartitionSpec as P

HEAD_DIM = 128
TOP = 2
GROUP = 4
MOST = 12
MESH = pl.DeviceIdType.MESH
BF = jnp.bfloat16
F32 = jnp.float32


def layer_kernel(
    experts,
    dp,
    q_in,
    k_in,
    v_in,
    index_in,
    gates_in,
    docs_in,
    cap_in,
    gain_in,
    wg_in,
    wu_in,
    wd_in,
    out,
    indexbuf,
    gatebuf,
    docbuf,
    capbuf,
    gainbuf,
    qbuf,
    kbuf,
    vbuf,
    metabuf,
    keyrow,
    keycol,
    docrow,
    pick,
    mix,
    att,
    sbuf,
    xbuf,
    hbuf,
    ybuf,
    rbuf,
    fbuf,
    wgf,
    wuf,
    wdf,
    small_sem,
    q_sem,
    kv_sem,
    halo_sem,
    meta_sem,
    next_sem,
    disp_sem,
    ret_sem,
    fin_sem,
    ring_sem,
    part_sem,
    own_sem,
    qkv_send,
    halo_send,
    meta_send,
    next_send,
    disp_send,
    ret_send,
    fin_send,
    w_send,
    entered,
):
    rows, width = q_in.shape
    cols = width // GROUP
    heads = cols // HEAD_DIM
    span = GROUP * rows
    slots = GROUP * MOST
    planes = experts // GROUP
    ring = dp // 2
    hops = ring // 2

    me = lax.axis_index("expert")
    z, x = lax.div(me, GROUP), lax.rem(me, GROUP)
    d = lax.axis_index("dp")
    y, core = lax.div(d, 2), lax.rem(d, 2)
    above = {"expert": lax.rem(z + 1, planes) * GROUP + x}
    below = {"expert": lax.rem(z + planes - 1, planes) * GROUP + x}
    up = {"dp": lax.rem(y + 1, ring) * 2 + core}
    down = {"dp": lax.rem(y + ring - 1, ring) * 2 + core}
    partner = {"dp": y * 2 + 1 - core}

    def mate(i):
        return lax.rem(x + i, GROUP)

    def in_group(peer):
        return {"expert": z * GROUP + peer}

    def at(start, size, unit):
        return pl.ds(pl.multiple_of(start, unit), size)

    def send(src, dst, send_sem, recv_sem, where):
        pltpu.make_async_remote_copy(
            src_ref=src, dst_ref=dst, send_sem=send_sem, recv_sem=recv_sem, device_id=where, device_id_type=MESH
        ).start()

    def local(src, dst, sem):
        pltpu.make_async_copy(src, dst, sem).start()

    def wait(ref, sem):
        pltpu.make_async_copy(ref, ref, sem).wait()

    barrier = pltpu.get_barrier_semaphore()
    near = [in_group(mate(i)) for i in range(1, GROUP)] + [above, below, up, down, partner]
    for other in near:
        pl.semaphore_signal(barrier, inc=1, device_id=other, device_id_type=MESH)
    small = ((index_in, indexbuf), (gates_in, gatebuf), (docs_in, docbuf), (cap_in, capbuf), (gain_in, gainbuf))
    for i, (source, buf) in enumerate(small):
        local(source, buf, small_sem.at[i])
    for i, (source, buf) in enumerate(small):
        wait(buf, small_sem.at[i])
    metabuf[GROUP + x, pl.ds(0, TOP), :] = indexbuf[...].astype(F32)
    metabuf[GROUP + x, pl.ds(TOP, TOP), :] = gatebuf[...]
    metabuf[GROUP + x, pl.ds(2 * TOP, 1), :] = docbuf[...].astype(F32)
    metabuf[GROUP + x, pl.ds(2 * TOP + 1, 3), :] = jnp.zeros((3, rows), F32)
    pl.semaphore_wait(barrier, len(near))

    own_rows = at(x * rows, rows, rows)
    own_late = at(span + x * rows, rows, rows)

    def head_at(peer, h):
        return at(peer * cols + h * HEAD_DIM, HEAD_DIM, HEAD_DIM)

    def give_keys(h):
        here = pl.ds(h * HEAD_DIM, HEAD_DIM)
        for i in range(1, GROUP):
            peer = mate(i)
            for n, (source, buf) in enumerate(((k_in, kbuf), (v_in, vbuf))):
                send(source.at[:, head_at(peer, h)], buf.at[own_late, here], qkv_send.at[n], kv_sem.at[h], in_group(peer))

    def give_queries(h):
        here = pl.ds(h * HEAD_DIM, HEAD_DIM)
        for i in range(1, GROUP):
            peer = mate(i)
            send(q_in.at[:, head_at(peer, h)], qbuf.at[own_rows, here], qkv_send.at[2], q_sem.at[h], in_group(peer))

    def give_own(h):
        here = pl.ds(h * HEAD_DIM, HEAD_DIM)
        for source, buf in ((k_in, kbuf), (v_in, vbuf)):
            send(source.at[:, head_at(x, h)], buf.at[own_rows, here], halo_send, halo_sem.at[h], above)

    weights = ((wg_in, wgf), (wu_in, wuf), (wd_in, wdf))

    def block_of(piece, number, half):
        size = weights[piece][0].shape[0]
        base = (number * 2 + core) * size
        if half is None:
            return at(base, size, size)
        return at(base + half * (size // 2), size // 2, size // 2)

    def half_at(step, way):
        return way if step == hops - 1 else None

    def begin(piece):
        w_in, w_full = weights[piece]
        size = w_in.shape[0]
        for way, to in ((0, up), (1, down)):
            half = half_at(0, way)
            source = w_in if half is None else w_in.at[pl.ds(half * (size // 2), size // 2)]
            send(source, w_full.at[block_of(piece, y, half)], w_send.at[piece], ring_sem.at[way, 0, piece], to)
        send(w_in, w_full.at[block_of(piece, y, None)], w_send.at[piece], part_sem.at[piece], partner)
        local(w_in, w_full.at[block_of(piece, y, None)], own_sem.at[piece])

    def relay(step, piece):
        w_full = weights[piece][1]
        for way, to in ((0, up), (1, down)):
            number = lax.rem(y + ring - step - 1, ring) if way == 0 else lax.rem(y + step + 1, ring)
            came = w_full.at[block_of(piece, number, half_at(step, way))]
            wait(came, ring_sem.at[way, step, piece])
            if step + 1 < hops:
                onward = w_full.at[block_of(piece, number, half_at(step + 1, way))]
                send(onward, onward, w_send.at[piece], ring_sem.at[way, step + 1, piece], to)
            send(came, came, w_send.at[piece], part_sem.at[piece], partner)

    pending = []
    for step in range(hops + 1):
        if step < hops:
            pending += [(step, 0), (step, 1)]
        if step == 0:
            pending.append(None)
        else:
            pending.append((step - 1, 2))

    def pump(count):
        for _ in range(count):
            if pending:
                event = pending.pop(0)
                if event is None:
                    begin(2)
                else:
                    relay(*event)

    give_keys(0)
    begin(0)
    give_own(0)
    for i in range(1, GROUP):
        mine = metabuf.at[GROUP + x]
        send(mine, mine, meta_send, meta_sem, in_group(mate(i)))
    begin(1)
    for h in range(1, heads):
        give_own(h)
        give_keys(h)
        give_queries(h - 1)
    give_queries(heads - 1)
    for h in range(heads):
        here = pl.ds(h * HEAD_DIM, HEAD_DIM)
        for source, buf, there, sem in (
            (k_in, kbuf, own_late, kv_sem),
            (v_in, vbuf, own_late, kv_sem),
            (q_in, qbuf, own_rows, q_sem),
        ):
            local(source.at[:, head_at(x, h)], buf.at[there, here], sem.at[h])

    for _ in range(planes // 2):
        pl.semaphore_signal(entered.at[0], inc=1, device_id=above, device_id_type=MESH)
        pl.semaphore_signal(entered.at[1], inc=1, device_id=below, device_id_type=MESH)
        pl.semaphore_wait(entered.at[0], 1)
        pl.semaphore_wait(entered.at[1], 1)

    def forward(h):
        here = pl.ds(h * HEAD_DIM, HEAD_DIM)
        wait(kbuf.at[:, here], kv_sem.at[h])
        for i in range(1, GROUP):
            peer = mate(i)
            for buf in (kbuf, vbuf):
                source = buf.at[at(span + peer * rows, rows, rows), here]
                send(source, buf.at[at(peer * rows, rows, rows), here], halo_send, halo_sem.at[h], above)

    forward(0)

    wait(metabuf.at[pl.ds(0, GROUP - 1)], meta_sem)
    send(metabuf.at[pl.ds(GROUP, GROUP)], metabuf.at[pl.ds(0, GROUP)], next_send, next_sem, above)
    number = lax.broadcasted_iota(jnp.int32, (experts, rows), 0).astype(F32)
    earlier = (
        lax.broadcasted_iota(jnp.int32, (rows, rows), 0) < lax.broadcasted_iota(jnp.int32, (rows, rows), 1)
    ).astype(BF)
    capacity = jnp.broadcast_to(capbuf[...].astype(F32), (8, experts)).astype(BF)
    for b in range(GROUP):
        block = metabuf[GROUP + b]
        lanes = pl.ds(b * rows, rows)
        chosen = [(block[k : k + 1, :] == number).astype(F32) for k in range(TOP)]
        before = jnp.dot((chosen[0] + chosen[1]).astype(BF), earlier, preferred_element_type=F32)
        for k in range(TOP):
            rank = jnp.sum(chosen[k] * before, axis=0, keepdims=True)
            limit = jnp.dot(capacity, chosen[k].astype(BF), preferred_element_type=F32)[0:1, :]
            key = jnp.where(rank < limit, block[k : k + 1, :] * slots + b * MOST + rank, -1.0)
            keyrow[pl.ds(k, 1), lanes] = key
        keyrow[pl.ds(2, 6), lanes] = block[2:8, :]
        docrow[pl.ds(0, 1), pl.ds(span + b * rows, rows)] = block[4:5, :]
        keycol[pl.ds(b * rows, rows), :] = jnp.transpose(keyrow[:, lanes])
    if heads > 1:
        forward(1)

    batch = min(8, experts)
    part = batch * slots

    def build_pick(g, carry):
        there = at(g * part, part, slots)
        row = (lax.broadcasted_iota(jnp.int32, (part, span), 0) + g * part).astype(F32)
        hit = (row == keyrow[0:1, :]) | (row == keyrow[1:2, :])
        pick[there, :] = hit.astype(F32).astype(BF)
        return carry

    lax.fori_loop(0, experts // batch, build_pick, 0)
    pump(1)

    def build_mix(b, carry):
        there = at(b * rows, rows, rows)
        slot = lax.broadcasted_iota(jnp.int32, (rows, experts * slots), 1).astype(F32)
        info = keycol[there, :]
        weight = jnp.where(slot == info[:, 0:1], info[:, 2:3], 0.0) + jnp.where(slot == info[:, 1:2], info[:, 3:4], 0.0)
        mix[there, :] = weight.astype(BF)
        return carry

    lax.fori_loop(0, GROUP, build_mix, 0)
    for h in range(2, heads):
        forward(h)
        pump(1)

    wait(metabuf.at[pl.ds(0, GROUP)], next_sem)
    first = jnp.where(z > 0, 1.0, 0.0)
    for b in range(GROUP):
        docrow[pl.ds(0, 1), pl.ds(b * rows, rows)] = (metabuf[b, pl.ds(4, 1), :] + 1.0) * first - 1.0

    i_row = lax.broadcasted_iota(jnp.int32, (rows, span + rows), 0)
    i_col = lax.broadcasted_iota(jnp.int32, (rows, span + rows), 1)
    band = (i_col > i_row) & (i_col <= i_row + span)
    scale = 1.0 / math.sqrt(HEAD_DIM)
    chunk = max(cols // 2, HEAD_DIM)
    for h in range(heads):
        lanes = pl.ds(h * HEAD_DIM, HEAD_DIM)
        wait(qbuf.at[:, lanes], q_sem.at[h])
        wait(kbuf.at[:, lanes], halo_sem.at[h])

        def attend(b, carry):
            there = at(b * rows, rows, rows)
            reach = at(b * rows, span + rows, rows)
            same = docrow[0:1, reach] == keycol[there, :][:, 4:5]
            bias = jnp.where(band & same, 0.0, -1e30)
            scores = lax.dot_general(
                qbuf[there, lanes], kbuf[reach, lanes], (((1,), (1,)), ((), ())), preferred_element_type=F32
            )
            scores = scores * scale + bias
            expo = jnp.exp(scores - jnp.max(scores, axis=-1, keepdims=True))
            probs = (expo * (1.0 / jnp.sum(expo, axis=-1, keepdims=True))).astype(BF)
            att[there, lanes] = jnp.dot(probs, vbuf[reach, lanes], preferred_element_type=F32).astype(BF)
            return carry

        lax.fori_loop(0, GROUP, attend, 0)
        if (h + 1) * HEAD_DIM % chunk:
            pump(1)
            continue
        c = (h + 1) * HEAD_DIM // chunk - 1
        here = pl.ds(c * chunk, chunk)

        def select(g, carry):
            there = at(g * part, part, slots)
            sbuf[there, here] = jnp.dot(pick[there, :], att[:, here], preferred_element_type=F32).astype(BF)
            return carry

        lax.fori_loop(0, experts // batch, select, 0)
        landing = xbuf.at[at(z * slots, slots, slots), at(x * cols + c * chunk, chunk, HEAD_DIM)]

        def dispatch(i, carry):
            e = lax.rem(me + i, experts)
            send(sbuf.at[at(e * slots, slots, slots), here], landing, disp_send, disp_sem.at[c], {"expert": e})
            return carry

        lax.fori_loop(1, experts, dispatch, 0)
        local(sbuf.at[at(me * slots, slots, slots), here], landing, disp_sem.at[c])
        pump(1)

    pump(len(pending) - 2)
    for c in range(cols // chunk):
        wait(rbuf.at[:, pl.ds(c * chunk, chunk)], disp_sem.at[c])

    gain = gainbuf[...]

    def normalise(g, carry):
        there = at(g * slots, slots, slots)
        row = xbuf[there, :].astype(F32)
        inverse = lax.rsqrt(jnp.sum(row * row, axis=-1, keepdims=True) * (1.0 / width) + 1e-05)
        xbuf[there, :] = (row * inverse * gain).astype(BF)
        return carry

    lax.fori_loop(0, planes, normalise, 0)
    for piece in range(2):
        wait(weights[piece][0], own_sem.at[piece])
        wait(weights[piece][1].at[pl.ds(0, width // 2)], part_sem.at[piece])
    hidden = wgf.shape[1]
    strip = min(256, hidden)

    def inner(n, carry):
        there = at(n * strip, strip, strip)
        gate = jnp.dot(xbuf[...], wgf[:, there], preferred_element_type=F32)
        upward = jnp.dot(xbuf[...], wuf[:, there], preferred_element_type=F32)
        hbuf[:, there] = (gate / (1.0 + jnp.exp(-gate)) * upward).astype(BF)
        return carry

    pump(1)
    strips = hidden // strip
    lax.fori_loop(0, strips - strips // 2, inner, 0)
    pump(len(pending))
    lax.fori_loop(strips - strips // 2, strips, inner, 0)
    wait(wd_in, own_sem.at[2])
    wait(wdf.at[pl.ds(0, hidden // 2)], part_sem.at[2])

    returns, start = [], 0
    while start < cols:
        size = max(HEAD_DIM, (cols // 2 if start == 0 else cols // 4) // HEAD_DIM * HEAD_DIM)
        returns.append((start, size))
        start += size
    for c, (start, size) in enumerate(returns):
        landing = rbuf.at[at(me * slots, slots, slots), pl.ds(start, size)]

        def outer(j, carry):
            peer = mate(1 + j)
            theirs = at(peer * cols + start, size, HEAD_DIM)
            ybuf[:, theirs] = jnp.dot(hbuf[...], wdf[:, theirs], preferred_element_type=F32).astype(BF)

            def give(i, inner_carry):
                plane = lax.rem(z + i, planes)
                e = plane * GROUP + peer
                source = ybuf.at[at(plane * slots, slots, slots), theirs]

                @pl.when(e != me)
                def _():
                    send(source, landing, ret_send, ret_sem.at[c], {"expert": e})

                @pl.when(e == me)
                def _():
                    local(source, landing, ret_sem.at[c])

                return inner_carry

            lax.fori_loop(0, planes, give, 0)
            return carry

        lax.fori_loop(0, GROUP, outer, 0)

    for c, (start, size) in enumerate(returns):
        here = pl.ds(start, size)
        wait(rbuf.at[:, here], ret_sem.at[c])
        landing = out.at[:, at(x * cols + start, size, HEAD_DIM)]

        def combine(j, carry):
            peer = mate(1 + j)
            there = at(peer * rows, rows, rows)
            total = att[there, here].astype(F32) + jnp.dot(mix[there, :], rbuf[:, here], preferred_element_type=F32)
            fbuf[there, here] = total.astype(BF)
            return carry

        lax.fori_loop(0, GROUP, combine, 0)
        for i in range(1, GROUP):
            peer = mate(i)
            send(fbuf.at[at(peer * rows, rows, rows), here], landing, fin_send, fin_sem, in_group(peer))
        local(fbuf.at[own_rows, here], landing, fin_sem)

    for i in range(3):
        wait(qbuf.at[pl.ds(0, span - rows), :], qkv_send.at[i])
        size = weights[i][0].shape[0]
        wait(weights[i][1].at[pl.ds(0, (dp - 1) * size)], w_send.at[i])
    wait(kbuf, halo_send)
    wait(metabuf.at[pl.ds(0, GROUP - 1)], meta_send)
    wait(metabuf.at[pl.ds(0, GROUP)], next_send)
    wait(rbuf.at[pl.ds(0, (experts - 1) * slots), :], disp_send)
    wait(rbuf.at[pl.ds(0, (experts - 1) * slots), :], ret_send)
    wait(qbuf.at[pl.ds(0, span - rows), :], fin_send)
    wait(out, fin_sem)


def per_device(
    experts,
    dp,
    queries,
    keys,
    values,
    doc_ids,
    expert_index,
    gates,
    capacity,
    norm_gain,
    gate_weight,
    up_weight,
    down_weight,
):
    rows, width = queries.shape[1:]
    hidden = gate_weight.shape[2]
    cols = width // GROUP
    span = GROUP * rows
    slots = GROUP * MOST
    heads = cols // HEAD_DIM
    hbm = pl.BlockSpec(memory_space=pl.ANY)
    dma = pltpu.SemaphoreType.DMA
    out = pl.pallas_call(
        functools.partial(layer_kernel, experts, dp),
        out_shape=jax.ShapeDtypeStruct((rows, width), BF),
        in_specs=[hbm] * 11,
        out_specs=hbm,
        scratch_shapes=[
            pltpu.VMEM((TOP, rows), jnp.int32),
            pltpu.VMEM((TOP, rows), F32),
            pltpu.VMEM((1, rows), jnp.int32),
            pltpu.VMEM((1, experts), jnp.int32),
            pltpu.VMEM((1, width), F32),
            pltpu.VMEM((span, cols), BF),
            pltpu.VMEM((2 * span, cols), BF),
            pltpu.VMEM((2 * span, cols), BF),
            pltpu.VMEM((2 * GROUP, 8, rows), F32),
            pltpu.VMEM((8, span), F32),
            pltpu.VMEM((span, 8), F32),
            pltpu.VMEM((8, 2 * span), F32),
            pltpu.VMEM((experts * slots, span), BF),
            pltpu.VMEM((span, experts * slots), BF),
            pltpu.VMEM((span, cols), BF),
            pltpu.VMEM((experts * slots, cols), BF),
            pltpu.VMEM((experts // GROUP * slots, width), BF),
            pltpu.VMEM((experts // GROUP * slots, hidden), BF),
            pltpu.VMEM((experts // GROUP * slots, width), BF),
            pltpu.VMEM((experts * slots, cols), BF),
            pltpu.VMEM((span, cols), BF),
            pltpu.VMEM((width, hidden), BF),
            pltpu.VMEM((width, hidden), BF),
            pltpu.VMEM((hidden, width), BF),
            dma((5,)),
            dma((heads,)),
            dma((heads,)),
            dma((heads,)),
            dma,
            dma,
            dma((2,)),
            dma((4,)),
            dma,
            dma((2, dp // 4, 3)),
            dma((3,)),
            dma((3,)),
            dma((3,)),
            dma,
            dma,
            dma,
            dma,
            dma,
            dma,
            dma((3,)),
            pltpu.SemaphoreType.REGULAR((2,)),
        ],
        compiler_params=pltpu.CompilerParams(
            collective_id=0, has_side_effects=True, vmem_limit_bytes=56 * 1024 * 1024
        ),
        name="layer",
    )(
        queries[0],
        keys[0],
        values[0],
        expert_index[0].T,
        gates[0].T,
        doc_ids,
        capacity[None, :],
        norm_gain[None, :],
        gate_weight[0],
        up_weight[0],
        down_weight[0],
    )
    return out[None]


def solution(mesh):
    placed = (
        P("dp", "expert", None),
        P("dp", "expert", None),
        P("dp", "expert", None),
        P("dp", "expert"),
        P("dp", "expert", None),
        P("dp", "expert", None),
        P(),
        P(),
        P("expert", "dp", None),
        P("expert", "dp", None),
        P("expert", "dp", None),
    )
    body = functools.partial(per_device, mesh.shape["expert"], mesh.shape["dp"])
    return jax.shard_map(body, mesh=mesh, in_specs=placed, out_specs=P("dp", "expert", None), check_vma=False)
```

time: 135 us -> 124 us (0.919)
  Pallas kernels: 128 us -> 121 us
  local copies, waits for them, and re-layouts: 5.22 us -> 1.88 us
    pallas_call x1, Pallas kernels: 128 us -> 121 us  [per_device(): pl.pallas_call(functools.partial(layer_kernel, experts, dp), out_shape=ja...]
    unnamed x9 -> x1, local copies, waits for them, and re-layouts: 4.47 us -> 1.88 us
where the time goes in v2:
time: 124 us; the launch traced here: 123 us
  Pallas kernels  121 us (98%)
  local copies, waits for them, and re-layouts  1.88 us (2%)
    pallas_call x1, Pallas kernels, per_device(): pl.pallas_call(functools.partial(layer_kernel, experts, dp), out_shape=ja...  121 us

profile of v2, /device:TPU:1, one launch (start us, length us, event | category | flops | bytes accessed | tf_op | source)
XLA Modules:
  0.0 123.3 jit_solution(17474773800186434343)
XLA Ops:
  0.0 121.4 %layer.1 = bf16[128,2048]{1,0:T(8,128)(2,1)} custom-call(bf16[128,2048]{1,0:T(8,128)(2,1)} %bitcast.16, bf16[128,2048]{1,0:T(8,128)(2,1)} %bitcast.17, bf16[128,2048]{1,0:T(8,128)(2,1)} %bitcast.18, s32[2,128]{1,0:T(2,128)} %bitcast.23, f32[2,128]{1,0:T(2,128)} %bitcast.24, s32[1,128]{1,0:T(1,128)} %docs_in.1, s32[1,32]{1,0:T(1,128)} %bitcast.25, ...), custom_call_target="tpu_custom_call" | custom-call | tf_op jit(solution)/shard_map/layer/pallas_call | solution.py:472
  121.4 1.9 %copy.13 = bf16[1,128,2048]{2,1,0:T(8,128)(2,1)} copy(bf16[1,128,2048]{2,1,0:T(8,128)(2,1)} %bitcast.15) | data formatting | bytes 1048576

commit v3 on v2

--- a/solution.py
+++ b/solution.py
@@ -135,8 +135,19 @@
     own_rows = at(x * rows, rows, rows)
     own_late = at(span + x * rows, rows, rows)
 
+    half_planes = planes // 2
+
+    def offset_of(place):
+        turn = planes - 1 - place
+        return lax.div(turn + 1, 2) * (2 * lax.rem(turn, 2) - 1)
+
+    def expert_at(i, side):
+        place = side * half_planes + lax.rem(i, half_planes)
+        plane = lax.rem(z + planes + offset_of(place), planes)
+        return place, plane * GROUP + mate(1 + lax.div(i, half_planes))
+
     def head_at(peer, h):
-        return at(peer * cols + h * HEAD_DIM, HEAD_DIM, HEAD_DIM)
+        return at((h * GROUP + peer) * HEAD_DIM, HEAD_DIM, HEAD_DIM)
 
     def give_keys(h):
         here = pl.ds(h * HEAD_DIM, HEAD_DIM)
@@ -156,11 +167,19 @@
         for source, buf in ((k_in, kbuf), (v_in, vbuf)):
             send(source.at[:, head_at(x, h)], buf.at[own_rows, here], halo_send, halo_sem.at[h], above)
 
-    weights = ((wg_in, wgf), (wu_in, wuf), (wd_in, wdf))
+    left, right = pl.ds(0, width // 2), pl.ds(width // 2, width // 2)
+    weights = (
+        (wg_in, wgf),
+        (wu_in, wuf),
+        (wd_in.at[:, left], wdf.at[:, left]),
+        (wd_in.at[:, right], wdf.at[:, right]),
+    )
 
     def block_of(piece, number, half):
         size = weights[piece][0].shape[0]
         base = (number * 2 + core) * size
+        if piece < 2:
+            base = (lax.rem(number * 2 + core, GROUP) * heads + lax.div(number * 2 + core, GROUP)) * size
         if half is None:
             return at(base, size, size)
         return at(base + half * (size // 2), size // 2, size // 2)
@@ -190,35 +209,58 @@
             send(came, came, w_send.at[piece], part_sem.at[piece], partner)
 
     pending = []
-    for step in range(hops + 1):
-        if step < hops:
-            pending += [(step, 0), (step, 1)]
-        if step == 0:
-            pending.append(None)
-        else:
-            pending.append((step - 1, 2))
+    for step in range(hops):
+        pending += [(step, 0), (step, 1)]
+        if step == hops - 2:
+            pending.append((-1, 3))
+        pending.append((step, 2))
+        if step == hops - 2:
+            pending.append((0, 3))
+    pending += [(step, 3) for step in range(1, hops)]
 
     def pump(count):
         for _ in range(count):
             if pending:
-                event = pending.pop(0)
-                if event is None:
-                    begin(2)
+                step, piece = pending.pop(0)
+                if step < 0:
+                    begin(piece)
                 else:
-                    relay(*event)
-
+                    relay(step, piece)
+
+    rounds = [planes // 2]
+
+    def announce():
+        pl.semaphore_signal(entered.at[0], inc=1, device_id=above, device_id_type=MESH)
+        pl.semaphore_signal(entered.at[1], inc=1, device_id=below, device_id_type=MESH)
+
+    def advance():
+        if rounds[0] == 0:
+            return
+        pl.semaphore_wait(entered.at[0], 1)
+        pl.semaphore_wait(entered.at[1], 1)
+        rounds[0] -= 1
+        if rounds[0] > 0:
+            announce()
+
+    early = min(2, heads)
+    announce()
     give_keys(0)
     begin(0)
-    give_own(0)
+    for h in range(heads):
+        give_own(h)
     for i in range(1, GROUP):
         mine = metabuf.at[GROUP + x]
         send(mine, mine, meta_send, meta_sem, in_group(mate(i)))
+    for h in range(1, early):
+        give_keys(h)
     begin(1)
-    for h in range(1, heads):
-        give_own(h)
+    for h in range(early):
+        give_queries(h)
+    begin(2)
+    for h in range(early, heads):
         give_keys(h)
-        give_queries(h - 1)
-    give_queries(heads - 1)
+    for h in range(early, heads):
+        give_queries(h)
     for h in range(heads):
         here = pl.ds(h * HEAD_DIM, HEAD_DIM)
         for source, buf, there, sem in (
@@ -227,12 +269,7 @@
             (q_in, qbuf, own_rows, q_sem),
         ):
             local(source.at[:, head_at(x, h)], buf.at[there, here], sem.at[h])
-
-    for _ in range(planes // 2):
-        pl.semaphore_signal(entered.at[0], inc=1, device_id=above, device_id_type=MESH)
-        pl.semaphore_signal(entered.at[1], inc=1, device_id=below, device_id_type=MESH)
-        pl.semaphore_wait(entered.at[0], 1)
-        pl.semaphore_wait(entered.at[1], 1)
+    advance()
 
     def forward(h):
         here = pl.ds(h * HEAD_DIM, HEAD_DIM)
@@ -244,6 +281,7 @@
                 send(source, buf.at[at(peer * rows, rows, rows), here], halo_send, halo_sem.at[h], above)
 
     forward(0)
+    advance()
 
     wait(metabuf.at[pl.ds(0, GROUP - 1)], meta_sem)
     send(metabuf.at[pl.ds(GROUP, GROUP)], metabuf.at[pl.ds(0, GROUP)], next_send, next_sem, above)
@@ -265,8 +303,10 @@
         keyrow[pl.ds(2, 6), lanes] = block[2:8, :]
         docrow[pl.ds(0, 1), pl.ds(span + b * rows, rows)] = block[4:5, :]
         keycol[pl.ds(b * rows, rows), :] = jnp.transpose(keyrow[:, lanes])
-    if heads > 1:
-        forward(1)
+    for h in range(1, early):
+        forward(h)
+    pump(1)
+    advance()
 
     batch = min(8, experts)
     part = batch * slots
@@ -279,7 +319,6 @@
         return carry
 
     lax.fori_loop(0, experts // batch, build_pick, 0)
-    pump(1)
 
     def build_mix(b, carry):
         there = at(b * rows, rows, rows)
@@ -290,9 +329,8 @@
         return carry
 
     lax.fori_loop(0, GROUP, build_mix, 0)
-    for h in range(2, heads):
-        forward(h)
-        pump(1)
+    while rounds[0]:
+        advance()
 
     wait(metabuf.at[pl.ds(0, GROUP)], next_sem)
     first = jnp.where(z > 0, 1.0, 0.0)
@@ -324,8 +362,11 @@
             return carry
 
         lax.fori_loop(0, GROUP, attend, 0)
+        if 0 < h < heads - 1:
+            pump(2)
+        if h + early < heads:
+            forward(h + early)
         if (h + 1) * HEAD_DIM % chunk:
-            pump(1)
             continue
         c = (h + 1) * HEAD_DIM // chunk - 1
         here = pl.ds(c * chunk, chunk)
@@ -336,105 +377,157 @@
             return carry
 
         lax.fori_loop(0, experts // batch, select, 0)
-        landing = xbuf.at[at(z * slots, slots, slots), at(x * cols + c * chunk, chunk, HEAD_DIM)]
-
-        def dispatch(i, carry):
-            e = lax.rem(me + i, experts)
-            send(sbuf.at[at(e * slots, slots, slots), here], landing, disp_send, disp_sem.at[c], {"expert": e})
+        last = h + 1 == heads
+        for side in (0, 1) if last else (0,):
+            for part_of in (c,) if side == 0 else range(c + 1):
+                there = pl.ds(part_of * chunk, chunk)
+                theirs = at(x * cols + part_of * chunk, chunk, HEAD_DIM)
+
+                def dispatch(i, carry):
+                    place, e = expert_at(i, side)
+                    send(
+                        sbuf.at[at(e * slots, slots, slots), there],
+                        xbuf.at[at(place * slots, slots, slots), theirs],
+                        disp_send,
+                        disp_sem.at[part_of, side],
+                        {"expert": e},
+                    )
+                    return carry
+
+                lax.fori_loop(0, GROUP * half_planes - side, dispatch, 0)
+                if side == 1:
+                    local(
+                        sbuf.at[at(me * slots, slots, slots), there],
+                        xbuf.at[pl.ds((planes - 1) * slots, slots), theirs],
+                        disp_sem.at[part_of, side],
+                    )
+        if not last:
+            pump(1)
+
+    pump(len(pending) - (hops - 1))
+
+    gain = jnp.concatenate(
+        [
+            gainbuf[:, pl.ds((h * GROUP + peer) * HEAD_DIM, HEAD_DIM)]
+            for peer in range(GROUP)
+            for h in range(heads)
+        ],
+        axis=1,
+    )
+    hidden = wgf.shape[1]
+    strip = min(256, hidden)
+    part_rows = half_planes * slots
+
+    def receive(side):
+        for c in range(cols // chunk):
+            wait(rbuf.at[pl.ds(0, experts // 2 * slots), pl.ds(c * chunk, chunk)], disp_sem.at[c, side])
+
+        def normalise(g, carry):
+            there = at(g * slots, slots, slots)
+            row = xbuf[there, :].astype(F32)
+            inverse = lax.rsqrt(jnp.sum(row * row, axis=-1, keepdims=True) * (1.0 / width) + 1e-05)
+            xbuf[there, :] = (row * inverse * gain).astype(BF)
             return carry
 
-        lax.fori_loop(1, experts, dispatch, 0)
-        local(sbuf.at[at(me * slots, slots, slots), here], landing, disp_sem.at[c])
+        lax.fori_loop(side * half_planes, (side + 1) * half_planes, normalise, 0)
+
+    def enter(side):
+        mine = pl.ds(side * part_rows, part_rows)
+
+        def inner(n, carry):
+            there = at(n * strip, strip, strip)
+            gate = jnp.dot(xbuf[mine, :], wgf[:, there], preferred_element_type=F32)
+            upward = jnp.dot(xbuf[mine, :], wuf[:, there], preferred_element_type=F32)
+            hbuf[mine, there] = (gate / (1.0 + jnp.exp(-gate)) * upward).astype(BF)
+            return carry
+
+        strips = hidden // strip
+        lax.fori_loop(0, strips - strips // 2, inner, 0)
         pump(1)
-
-    pump(len(pending) - 2)
-    for c in range(cols // chunk):
-        wait(rbuf.at[:, pl.ds(c * chunk, chunk)], disp_sem.at[c])
-
-    gain = gainbuf[...]
-
-    def normalise(g, carry):
-        there = at(g * slots, slots, slots)
-        row = xbuf[there, :].astype(F32)
-        inverse = lax.rsqrt(jnp.sum(row * row, axis=-1, keepdims=True) * (1.0 / width) + 1e-05)
-        xbuf[there, :] = (row * inverse * gain).astype(BF)
-        return carry
-
-    lax.fori_loop(0, planes, normalise, 0)
+        lax.fori_loop(strips - strips // 2, strips, inner, 0)
+
+    split = max(heads // 2, 1)
+    returns = [(0, split)] + [(h, 1) for h in range(split, heads)]
+
+    def leave(side, c):
+        first_head, count = returns[c]
+        start, size = first_head * HEAD_DIM, count * HEAD_DIM
+        mine = pl.ds(side * part_rows, part_rows)
+        landing = rbuf.at[at(me * slots, slots, slots), pl.ds(start, size)]
+        for h in range(first_head, first_head + count):
+            block = wdf[:, pl.ds(h * GROUP * HEAD_DIM, GROUP * HEAD_DIM)]
+            result = jnp.dot(hbuf[mine, :], block, preferred_element_type=F32).astype(BF)
+            for peer in range(GROUP):
+                ybuf[mine, pl.ds(peer * cols + h * HEAD_DIM, HEAD_DIM)] = result[:, peer * HEAD_DIM : (peer + 1) * HEAD_DIM]
+
+        def outer(j, carry):
+            peer = mate(1 + j)
+            theirs = at(peer * cols + start, size, HEAD_DIM)
+
+            def give(i, inner_carry):
+                place = side * half_planes + i
+                plane = lax.rem(z + planes - offset_of(place), planes)
+                e = plane * GROUP + peer
+                source = ybuf.at[at(place * slots, slots, slots), theirs]
+
+                @pl.when(e != me)
+                def _():
+                    send(source, landing, ret_send, ret_sem.at[c], {"expert": e})
+
+                @pl.when(e == me)
+                def _():
+                    local(source, landing, ret_sem.at[c])
+
+                return inner_carry
+
+            lax.fori_loop(0, half_planes, give, 0)
+            return carry
+
+        lax.fori_loop(0, GROUP, outer, 0)
+
+    receive(0)
     for piece in range(2):
         wait(weights[piece][0], own_sem.at[piece])
         wait(weights[piece][1].at[pl.ds(0, width // 2)], part_sem.at[piece])
-    hidden = wgf.shape[1]
-    strip = min(256, hidden)
-
-    def inner(n, carry):
-        there = at(n * strip, strip, strip)
-        gate = jnp.dot(xbuf[...], wgf[:, there], preferred_element_type=F32)
-        upward = jnp.dot(xbuf[...], wuf[:, there], preferred_element_type=F32)
-        hbuf[:, there] = (gate / (1.0 + jnp.exp(-gate)) * upward).astype(BF)
-        return carry
-
+    enter(0)
+    for piece in (2, 3):
+        wait(weights[piece][0], own_sem.at[piece])
+    wait(wdf.at[pl.ds(0, hidden // 2), left], part_sem.at[2])
+    leave(0, 0)
     pump(1)
-    strips = hidden // strip
-    lax.fori_loop(0, strips - strips // 2, inner, 0)
+    receive(1)
+    enter(1)
+    leave(1, 0)
     pump(len(pending))
-    lax.fori_loop(strips - strips // 2, strips, inner, 0)
-    wait(wd_in, own_sem.at[2])
-    wait(wdf.at[pl.ds(0, hidden // 2)], part_sem.at[2])
-
-    returns, start = [], 0
-    while start < cols:
-        size = max(HEAD_DIM, (cols // 2 if start == 0 else cols // 4) // HEAD_DIM * HEAD_DIM)
-        returns.append((start, size))
-        start += size
-    for c, (start, size) in enumerate(returns):
-        landing = rbuf.at[at(me * slots, slots, slots), pl.ds(start, size)]
-
-        def outer(j, carry):
-            peer = mate(1 + j)
-            theirs = at(peer * cols + start, size, HEAD_DIM)
-            ybuf[:, theirs] = jnp.dot(hbuf[...], wdf[:, theirs], preferred_element_type=F32).astype(BF)
-
-            def give(i, inner_carry):
-                plane = lax.rem(z + i, planes)
-                e = plane * GROUP + peer
-                source = ybuf.at[at(plane * slots, slots, slots), theirs]
-
-                @pl.when(e != me)
-                def _():
-                    send(source, landing, ret_send, ret_sem.at[c], {"expert": e})
-
-                @pl.when(e == me)
-                def _():
-                    local(source, landing, ret_sem.at[c])
-
-                return inner_carry
-
-            lax.fori_loop(0, planes, give, 0)
-            return carry
-
-        lax.fori_loop(0, GROUP, outer, 0)
-
-    for c, (start, size) in enumerate(returns):
-        here = pl.ds(start, size)
+    wait(wdf.at[pl.ds(0, hidden // 2), right], part_sem.at[3])
+    for c in range(1, len(returns)):
+        for side in range(2):
+            leave(side, c)
+
+    for c, (first_head, count) in enumerate(returns):
+        here = pl.ds(first_head * HEAD_DIM, count * HEAD_DIM)
+        finished = [(h, pl.ds(h * HEAD_DIM, HEAD_DIM)) for h in range(first_head, first_head + count)]
         wait(rbuf.at[:, here], ret_sem.at[c])
-        landing = out.at[:, at(x * cols + start, size, HEAD_DIM)]
-
-        def combine(j, carry):
-            peer = mate(1 + j)
-            there = at(peer * rows, rows, rows)
+
+        def hand_over(peer):
+            for h, lanes in finished:
+                source = fbuf.at[at(peer * rows, rows, rows), lanes]
+                send(source, out.at[:, head_at(x, h)], fin_send, fin_sem, in_group(peer))
+
+        ready = None
+        for i in (GROUP // 2, *(n for n in range(1, GROUP) if n != GROUP // 2), 0):
+            there = at(mate(i) * rows, rows, rows)
             total = att[there, here].astype(F32) + jnp.dot(mix[there, :], rbuf[:, here], preferred_element_type=F32)
             fbuf[there, here] = total.astype(BF)
-            return carry
-
-        lax.fori_loop(0, GROUP, combine, 0)
-        for i in range(1, GROUP):
-            peer = mate(i)
-            send(fbuf.at[at(peer * rows, rows, rows), here], landing, fin_send, fin_sem, in_group(peer))
-        local(fbuf.at[own_rows, here], landing, fin_sem)
+            if ready is not None:
+                hand_over(ready)
+            ready = mate(i)
+        for h, lanes in finished:
+            local(fbuf.at[own_rows, lanes], out.at[:, head_at(x, h)], fin_sem)
 
     for i in range(3):
         wait(qbuf.at[pl.ds(0, span - rows), :], qkv_send.at[i])
+    for i in range(4):
         size = weights[i][0].shape[0]
         wait(weights[i][1].at[pl.ds(0, (dp - 1) * size)], w_send.at[i])
     wait(kbuf, halo_send)
@@ -505,20 +598,20 @@
             dma((heads,)),
             dma,
             dma,
-            dma((2,)),
+            dma((2, 2)),
             dma((4,)),
             dma,
-            dma((2, dp // 4, 3)),
+            dma((2, dp // 4, 4)),
+            dma((4,)),
+            dma((4,)),
             dma((3,)),
-            dma((3,)),
-            dma((3,)),
-            dma,
-            dma,
-            dma,
-            dma,
-            dma,
-            dma,
-            dma((3,)),
+            dma,
+            dma,
+            dma,
+            dma,
+            dma,
+            dma,
+            dma((4,)),
             pltpu.SemaphoreType.REGULAR((2,)),
         ],
         compiler_params=pltpu.CompilerParams(

time: 124 us -> 116 us (0.935)
  Pallas kernels: 121 us -> 114 us
    pallas_call x1, Pallas kernels: 121 us -> 114 us  [per_device(): pl.pallas_call(functools.partial(layer_kernel, experts, dp), out_shape=ja...]
where the time goes in v3:
time: 116 us
  Pallas kernels  114 us (98%)
  local copies, waits for them, and re-layouts  1.88 us (2%)
    pallas_call x1, Pallas kernels, per_device(): pl.pallas_call(functools.partial(layer_kernel, experts, dp), out_shape=ja...  114 us

profile of v3, /device:TPU:1, one launch (start us, length us, event | category | flops | bytes accessed | tf_op | source)
XLA Modules:
  0.0 115.5 jit_solution(13252889690085954574)
XLA Ops:
  0.0 113.7 %layer.1 = bf16[128,2048]{1,0:T(8,128)(2,1)} custom-call(bf16[128,2048]{1,0:T(8,128)(2,1)} %bitcast.16, bf16[128,2048]{1,0:T(8,128)(2,1)} %bitcast.17, bf16[128,2048]{1,0:T(8,128)(2,1)} %bitcast.18, s32[2,128]{1,0:T(2,128)} %bitcast.23, f32[2,128]{1,0:T(2,128)} %bitcast.24, s32[1,128]{1,0:T(1,128)} %docs_in.1, s32[1,32]{1,0:T(1,128)} %bitcast.25, ...), custom_call_target="tpu_custom_call" | custom-call | tf_op jit(solution)/shard_map/layer/pallas_call | solution.py:565
  113.7 1.9 %copy.13 = bf16[1,128,2048]{2,1,0:T(8,128)(2,1)} copy(bf16[1,128,2048]{2,1,0:T(8,128)(2,1)} %bitcast.15) | data formatting | bytes 1048576

commit v4 on v3

--- a/solution.py
+++ b/solution.py
@@ -210,13 +210,10 @@
 
     pending = []
     for step in range(hops):
-        pending += [(step, 0), (step, 1)]
+        pending += [(step, 0), (step, 1), (step, 2)]
         if step == hops - 2:
             pending.append((-1, 3))
-        pending.append((step, 2))
-        if step == hops - 2:
-            pending.append((0, 3))
-    pending += [(step, 3) for step in range(1, hops)]
+    pending += [(step, 3) for step in range(hops)]
 
     def pump(count):
         for _ in range(count):
@@ -404,7 +401,7 @@
         if not last:
             pump(1)
 
-    pump(len(pending) - (hops - 1))
+    pump(len(pending) - hops)
 
     gain = jnp.concatenate(
         [
@@ -564,9 +561,9 @@
     dma = pltpu.SemaphoreType.DMA
     out = pl.pallas_call(
         functools.partial(layer_kernel, experts, dp),
-        out_shape=jax.ShapeDtypeStruct((rows, width), BF),
+        out_shape=pltpu.VMEM((rows, width), BF),
         in_specs=[hbm] * 11,
-        out_specs=hbm,
+        out_specs=pl.BlockSpec(memory_space=pltpu.VMEM),
         scratch_shapes=[
             pltpu.VMEM((TOP, rows), jnp.int32),
             pltpu.VMEM((TOP, rows), F32),

time: 116 us -> 112 us (0.966)
  Pallas kernels: 114 us -> 111 us
    pallas_call x1, Pallas kernels: 114 us -> 111 us  [per_device(): pl.pallas_call(functools.partial(layer_kernel, experts, dp), out_shape=pl...]
where the time goes in v4:
time: 112 us
  Pallas kernels  111 us (99%)
    pallas_call x1, Pallas kernels, per_device(): pl.pallas_call(functools.partial(layer_kernel, experts, dp), out_shape=pl...  111 us

profile of v4, /device:TPU:1, one launch (start us, length us, event | category | flops | bytes accessed | tf_op | source)
XLA Modules:
  0.0 111.7 jit_solution(1883770401549729268)
XLA Ops:
  0.0 110.9 %layer.1 = bf16[128,2048]{1,0:T(8,128)(2,1)S(1)} custom-call(bf16[128,2048]{1,0:T(8,128)(2,1)} %bitcast.16, bf16[128,2048]{1,0:T(8,128)(2,1)} %bitcast.17, bf16[128,2048]{1,0:T(8,128)(2,1)} %bitcast.18, s32[2,128]{1,0:T(2,128)} %bitcast.23, f32[2,128]{1,0:T(2,128)} %bitcast.24, s32[1,128]{1,0:T(1,128)} %docs_in.1, s32[1,32]{1,0:T(1,128)} %bitcast.25, ...), custom_call_target="tpu_custom_call" | custom-call | tf_op jit(solution)/shard_map/layer/pallas_call | solution.py:562
  110.9 0.8 copy.13

commit v5 on v4

--- a/solution.py
+++ b/solution.py
@@ -124,12 +124,6 @@
     small = ((index_in, indexbuf), (gates_in, gatebuf), (docs_in, docbuf), (cap_in, capbuf), (gain_in, gainbuf))
     for i, (source, buf) in enumerate(small):
         local(source, buf, small_sem.at[i])
-    for i, (source, buf) in enumerate(small):
-        wait(buf, small_sem.at[i])
-    metabuf[GROUP + x, pl.ds(0, TOP), :] = indexbuf[...].astype(F32)
-    metabuf[GROUP + x, pl.ds(TOP, TOP), :] = gatebuf[...]
-    metabuf[GROUP + x, pl.ds(2 * TOP, 1), :] = docbuf[...].astype(F32)
-    metabuf[GROUP + x, pl.ds(2 * TOP + 1, 3), :] = jnp.zeros((3, rows), F32)
     pl.semaphore_wait(barrier, len(near))
 
     own_rows = at(x * rows, rows, rows)
@@ -241,13 +235,16 @@
 
     early = min(2, heads)
     announce()
+    begin(0)
     give_keys(0)
-    begin(0)
     for h in range(heads):
         give_own(h)
-    for i in range(1, GROUP):
-        mine = metabuf.at[GROUP + x]
-        send(mine, mine, meta_send, meta_sem, in_group(mate(i)))
+    for i, (source, buf) in enumerate(small):
+        wait(buf, small_sem.at[i])
+    metabuf[GROUP + x, pl.ds(0, TOP), :] = indexbuf[...].astype(F32)
+    metabuf[GROUP + x, pl.ds(TOP, TOP), :] = gatebuf[...]
+    metabuf[GROUP + x, pl.ds(2 * TOP, 1), :] = docbuf[...].astype(F32)
+    metabuf[GROUP + x, pl.ds(2 * TOP + 1, 3), :] = jnp.zeros((3, rows), F32)
     for h in range(1, early):
         give_keys(h)
     begin(1)
@@ -258,6 +255,9 @@
         give_keys(h)
     for h in range(early, heads):
         give_queries(h)
+    for i in range(1, GROUP):
+        mine = metabuf.at[GROUP + x]
+        send(mine, mine, meta_send, meta_sem, in_group(mate(i)))
     for h in range(heads):
         here = pl.ds(h * HEAD_DIM, HEAD_DIM)
         for source, buf, there, sem in (

time: 112 us -> 121 us (1.080); the launches traced: 112 us -> 119 us
  Pallas kernels: 111 us -> 118 us
    pallas_call x1, Pallas kernels: 111 us -> 118 us  [per_device(): pl.pallas_call(functools.partial(layer_kernel, experts, dp), out_shape=pl...]
where the time goes in v5:
time: 121 us; the launch traced here: 119 us
  Pallas kernels  118 us (98%)
    pallas_call x1, Pallas kernels, per_device(): pl.pallas_call(functools.partial(layer_kernel, experts, dp), out_shape=pl...  118 us

profile of v5, /device:TPU:1, one launch (start us, length us, event | category | flops | bytes accessed | tf_op | source)
XLA Modules:
  0.0 118.5 jit_solution(13533556407934472853)
XLA Ops:
  0.0 117.7 %layer.1 = bf16[128,2048]{1,0:T(8,128)(2,1)S(1)} custom-call(bf16[128,2048]{1,0:T(8,128)(2,1)} %bitcast.16, bf16[128,2048]{1,0:T(8,128)(2,1)} %bitcast.17, bf16[128,2048]{1,0:T(8,128)(2,1)} %bitcast.18, s32[2,128]{1,0:T(2,128)} %bitcast.23, f32[2,128]{1,0:T(2,128)} %bitcast.24, s32[1,128]{1,0:T(1,128)} %docs_in.1, s32[1,32]{1,0:T(1,128)} %bitcast.25, ...), custom_call_target="tpu_custom_call" | custom-call | tf_op jit(solution)/shard_map/layer/pallas_call | solution.py:562
  117.7 0.8 copy.13
